TPU v7x, 32 devices: a whole 2x2x4 slice. The times are simulated.
32 devices in a mesh: phase: 16 (over z, y, x), lat: 2 (over core).
Axes of the slice: x: 2, y: 2, z: 4, core: 2. Of those that a mesh axis runs over, the one named last changes fastest.
Arguments:
- state_now: float32 [3, 64, 1024], P(None, ('lat', 'phase')), may hold values from -4 to 4
- ocean_depth: float32 [64, 1024], P('lat'), may hold values from 0.5 to 1.5
- coriolis: float32 [64], P('lat'), may hold values from -0.4 to 0.4
- phase_times: float32 [16], P('phase'), may hold values from -6 to 6
- phase_weights: float32 [16], P('phase'), may hold values from 0.00625 to 0.25
Outputs:
- state_next: float32 [3, 64, 1024], P(None, ('lat', 'phase'))
- tendency: float32 [3, 64, 1024], P(None, ('lat', 'phase'))
All inputs are finite; a program needn't handle non-finite values.
Results may differ from a plain program's by a relative error of at most 0.00002.
Values sent between devices are 32-bit elements; how exact they have to be, the bound alone decides.
A program may use at most 64 MiB of HBM per device.

v0:
```python
import math
import jax
import jax.numpy as jnp
from jax import lax
from jax.sharding import PartitionSpec as P

DEG = 8
DEPTH = 4
radius_scale = 2.5
time_step = 0.5
series_terms = 20


def extended(shard, sides, width):
    for axis, dim in sides:
        devices, length = (lax.axis_size(axis), shard.shape[dim])
        up = [(i, (i + 1) % devices) for i in range(devices - 1)]
        down = [(j, i) for i, j in up]
        last = lax.slice_in_dim(shard, length - width, length, axis=dim)
        first = lax.slice_in_dim(shard, 0, width, axis=dim)
        before = lax.ppermute(last, axis, up)
        after = lax.ppermute(first, axis, down)
        shard = jnp.concatenate([before, shard, after], axis=dim)
    return shard


def along_lon(values):
    return (jnp.roll(values, -1, axis=-1) - jnp.roll(values, 1, axis=-1)) * 0.5


def along_lat(values):
    return (values[..., 2:, :] - values[..., :-2, :]) * 0.5


def interior(values):
    return values[..., 1:-1, :]


def wave_operator(fields, coefficients):
    height = fields[:, 0]
    eastward = fields[:, 1]
    northward = fields[:, 2]
    depth_field = coefficients[0]
    rotation = coefficients[1]
    out_height = -(along_lon(interior(depth_field * eastward)) + along_lat(depth_field * northward))
    out_east = -along_lon(interior(height)) + interior(rotation * northward)
    out_north = -along_lat(height) - interior(rotation * eastward)
    return jnp.stack([out_height, out_east, out_north], axis=1) / radius_scale


def advection(fields):
    height = fields[:, 0]
    eastward = fields[:, 1]
    northward = fields[:, 2]
    mid_east = interior(eastward)
    mid_north = interior(northward)
    out_height = -(along_lon(interior(height * eastward)) + along_lat(height * northward))
    out_east = -(mid_east * along_lon(mid_east) + mid_north * along_lat(eastward))
    out_north = -(mid_east * along_lon(mid_north) + mid_north * along_lat(northward))
    return jnp.stack([out_height, out_east, out_north], axis=1)


def series_coeffs(sample_time):
    half_time = sample_time * 0.5
    square = half_time * half_time
    result = []
    for degree in range(DEG + 1):
        summed = jnp.zeros_like(sample_time)
        term_sq = jnp.ones_like(sample_time)
        for series in range(series_terms):
            factor = (-1.0) ** series / (math.factorial(series) * math.factorial(series + degree))
            summed = summed + factor * term_sq
            term_sq = term_sq * square
        result.append(summed * half_time**degree)
    return result


def trimmed(values, have, wanted):
    excess = have - wanted
    if excess == 0:
        return values
    return values[:, :, excess : values.shape[2] - excess]


def per_device(state_now, ocean_depth, coriolis, phase_times, phase_weights):
    tile_rows = ocean_depth.shape[0]
    lat_count = lax.axis_size("lat")
    lat_place = lax.axis_index("lat")
    stacked = jnp.stack([ocean_depth, jnp.broadcast_to(coriolis[:, None], ocean_depth.shape)])
    coefficients = extended(stacked, (("lat", 1),), DEPTH)
    global_rows = lat_place * tile_rows - DEPTH + jnp.arange(tile_rows + 2 * DEPTH, dtype=jnp.int32)
    inside = ((global_rows >= 0) & (global_rows < tile_rows * lat_count)).astype(jnp.float32)
    forward = series_coeffs(phase_times)
    backward = series_coeffs(-phase_times)
    sample_count = phase_times.shape[0]

    def band_coeffs(margin):
        return coefficients[:, DEPTH - margin : DEPTH + tile_rows + margin]

    def band_inside(margin):
        return inside[DEPTH - margin : DEPTH + tile_rows + margin][None, None, :, None]

    def exponential(fields, series):
        accumulated = series[0][:, None, None, None] * fields
        previous = None
        current = fields
        width_prev = 0
        width_cur = 0
        for degree in range(1, DEG + 1):
            if (degree - 1) % DEPTH == 0:
                if previous is None:
                    current = extended(current, (("lat", 2),), DEPTH)
                else:
                    joined = jnp.concatenate(
                        [trimmed(previous, width_prev, 0), trimmed(current, width_cur, 0)], axis=0
                    )
                    joined = extended(joined, (("lat", 2),), DEPTH)
                    previous = joined[:sample_count]
                    current = joined[sample_count:]
                    width_prev = DEPTH
                width_cur = DEPTH
            width_new = width_cur - 1
            applied = wave_operator(current, band_coeffs(width_cur))
            if previous is None:
                advanced = applied
            else:
                advanced = 2.0 * applied + trimmed(previous, width_prev, width_new)
            advanced = advanced * band_inside(width_new)
            accumulated = accumulated + 2.0 * series[degree][:, None, None, None] * trimmed(
                advanced, width_new, 0
            )
            previous = current
            width_prev = width_cur
            current = advanced
            width_cur = width_new
        return accumulated

    def averaged(whole_tile):
        samples = whole_tile[None]
        waves = exponential(samples, forward)
        rimmed = extended(waves, (("lat", 2),), 1)
        pulled = advection(rimmed)
        returned = exponential(pulled, backward)
        return jnp.sum(phase_weights[:, None, None, None] * returned, axis=0)

    whole_tile = lax.all_gather(state_now, "phase", axis=1, tiled=True)

    def summed_whole(partial_value):
        return lax.psum(partial_value, "phase")

    first = summed_whole(averaged(whole_tile))
    middle = whole_tile + time_step * first
    second = summed_whole(averaged(middle))
    tendency_tile = 0.5 * (first + second)
    share = state_now.shape[1]
    start = lax.axis_index("phase") * share
    tendency = lax.dynamic_slice_in_dim(tendency_tile, start, share, 1)
    state_next = state_now + time_step * tendency
    return (state_next, tendency)


def solution(mesh):
    placed = (P(None, ("lat", "phase"), None), P("lat", None), P("lat"), P("phase"), P("phase"))
    return jax.shard_map(
        per_device,
        mesh=mesh,
        in_specs=placed,
        out_specs=(P(None, ("lat", "phase"), None), P(None, ("lat", "phase"), None)),
        check_vma=False,
    )
```

profile of v0, /device:TPU:0, one launch (start us, length us, event | category | flops | bytes accessed | tf_op | source)
XLA Modules:
  0.0 368.3 jit_solution(13352655160559666389)
XLA Ops:
  8.0 45.3 %all_gather.3 = f32[3,32,1024]{2,0,1:T(4,128)S(1)} all-gather(f32[3,2,1024]{2,0,1:T(4,128)S(1)} %copy.168), channel_id=1, replica_groups=mesh['phase'=16,'lat'=2] {'phase'}, dimensions={1}, use_global_device_ids=true | all-gather | bytes 417792 | tf_op jit(solution)/shard_map/all_gather | solution.py:146
  53.6 1.4 collective-permute-start.3
  55.0 3.0 collective-permute-start.2
  58.2 1.3 collective-permute-start.1
  59.5 3.0 collective-permute-start
  67.0 1.3 collective-permute-start.5
  68.3 3.0 collective-permute-start.4
  76.5 1.3 collective-permute-start.7
  77.8 3.0 collective-permute-start.6
  82.7 1.3 collective-permute-start.9
  84.0 3.0 collective-permute-start.8
  91.5 1.3 collective-permute-start.11
  92.8 3.2 collective-permute-start.10
  100.2 1.3 fusion.41
  101.6 104.9 %all-reduce.3.cloned.1.call-done = f32[3,32,1024]{2,1,0:T(8,128)} async-done(((f32[3,32,1024]{2,1,0:T(8,128)}), f32[3,32,1024]{2,1,0:T(8,128)}) %all-reduce.3.cloned.1.call-update) | async-done | bytes 393232 | tf_op jit(solution)/shard_map/psum | solution.py:149
  207.8 1.3 collective-permute-start.13
  209.1 3.0 collective-permute-start.12
  217.9 3.0 collective-permute-start.14
  228.3 3.0 collective-permute-start.16
  233.2 1.3 collective-permute-start.19
  234.5 3.3 collective-permute-start.18
  243.2 3.0 collective-permute-start.20
  252.0 107.9 %all-reduce.5.cloned.1.call-done = f32[3,32,1024]{2,1,0:T(8,128)} async-done(((f32[3,32,1024]{2,1,0:T(8,128)}), f32[3,32,1024]{2,1,0:T(8,128)}) %all-reduce.5.cloned.1.call-update) | async-done | bytes 393232 | tf_op jit(solution)/shard_map/psum | solution.py:149
  359.9 1.5 multiply_add_fusion.1
  (380 shorter events, 45.4 us)
Async XLA Ops:
  7.2 199.3 %all-reduce.3.cloned.1.call-start = ((), (), s32[]{:S(2)}) async-start(), calls=%async_computation | async-start | bytes 786432 | tf_op jit(solution)/shard_map/psum | solution.py:149
  53.6 9.8 %collective-permute-start.3 = (f32[1,3,4,1024]{3,2,1,0:T(4,128)S(1)}, f32[1,3,4,1024]{3,2,1,0:T(4,128)S(1)}, u32[]{:S(2)}, u32[]{:S(2)}) collective-permute-start(f32[1,3,4,1024]{3,2,1,0:T(4,128)S(1)} %get-tuple-element.195), channel_id=1, source_target_pairs={{1,0},{3,2},{5,4},{7,6},{9,8},{11,10},{13,12},{15,14},{17,16},{19,... | collective-permute-start | bytes 147464 | tf_op jit(solution)/shard_map/ppermute | solution.py:22
  55.0 8.4 %collective-permute-start.2 = (f32[1,3,4,1024]{3,2,1,0:T(4,128)S(1)}, f32[1,3,4,1024]{3,2,1,0:T(4,128)S(1)}, u32[]{:S(2)}, u32[]{:S(2)}) collective-permute-start(f32[1,3,4,1024]{3,2,1,0:T(4,128)S(1)} %get-tuple-element.194), channel_id=1, source_target_pairs={{0,1},{2,3},{4,5},{6,7},{8,9},{10,11},{12,13},{14,15},{16,17},{18,... | collective-permute-start | bytes 147464 | tf_op jit(solution)/shard_map/ppermute | solution.py:21
  58.2 4.6 %collective-permute-start.1 = (f32[2,4,1024]{2,1,0:T(4,128)S(1)}, f32[2,4,1024]{2,1,0:T(4,128)S(1)}, u32[]{:S(2)}, u32[]{:S(2)}) collective-permute-start(f32[2,4,1024]{2,1,0:T(4,128)S(1)} %get-tuple-element.205), channel_id=1, source_target_pairs={{1,0},{3,2},{5,4},{7,6},{9,8},{11,10},{13,12},{15,14},{17,16},{19,... | collective-permute-start | bytes 98312 | tf_op jit(solution)/shard_map/ppermute | solution.py:22
  59.5 3.9 %collective-permute-start = (f32[2,4,1024]{2,1,0:T(4,128)S(1)}, f32[2,4,1024]{2,1,0:T(4,128)S(1)}, u32[]{:S(2)}, u32[]{:S(2)}) collective-permute-start(f32[2,4,1024]{2,1,0:T(4,128)S(1)} %get-tuple-element.204), channel_id=1, source_target_pairs={{0,1},{2,3},{4,5},{6,7},{8,9},{10,11},{12,13},{14,15},{16,17},{18,... | collective-permute-start | bytes 98312 | tf_op jit(solution)/shard_map/ppermute | solution.py:21
  67.0 5.3 %collective-permute-start.5 = (f32[2,3,4,1024]{3,2,1,0:T(4,128)S(1)}, f32[2,3,4,1024]{3,2,1,0:T(4,128)S(1)}, u32[]{:S(2)}, u32[]{:S(2)}) collective-permute-start(f32[2,3,4,1024]{3,2,1,0:T(4,128)S(1)} %get-tuple-element.91), channel_id=1, source_target_pairs={{1,0},{3,2},{5,4},{7,6},{9,8},{11,10},{13,12},{15,14},{17,16},{19,... | collective-permute-start | bytes 294920 | tf_op jit(solution)/shard_map/ppermute | solution.py:22
  68.3 4.0 %collective-permute-start.4 = (f32[2,3,4,1024]{3,2,1,0:T(4,128)S(1)}, f32[2,3,4,1024]{3,2,1,0:T(4,128)S(1)}, u32[]{:S(2)}, u32[]{:S(2)}) collective-permute-start(f32[2,3,4,1024]{3,2,1,0:T(4,128)S(1)} %get-tuple-element.90), channel_id=1, source_target_pairs={{0,1},{2,3},{4,5},{6,7},{8,9},{10,11},{12,13},{14,15},{16,17},{18,... | collective-permute-start | bytes 294920 | tf_op jit(solution)/shard_map/ppermute | solution.py:21
  76.5 4.3 %collective-permute-start.7 = (f32[1,3,1,1024]{3,2,1,0:T(1,128)S(1)}, f32[1,3,1,1024]{3,2,1,0:T(1,128)S(1)}, u32[]{:S(2)}, u32[]{:S(2)}) collective-permute-start(f32[1,3,1,1024]{3,2,1,0:T(1,128)S(1)} %get-tuple-element.193), channel_id=1, source_target_pairs={{1,0},{3,2},{5,4},{7,6},{9,8},{11,10},{13,12},{15,14},{17,16},{19,... | collective-permute-start | bytes 36872 | tf_op jit(solution)/shard_map/ppermute | solution.py:22
  77.8 3.9 %collective-permute-start.6 = (f32[1,3,1,1024]{3,2,1,0:T(1,128)S(1)}, f32[1,3,1,1024]{3,2,1,0:T(1,128)S(1)}, u32[]{:S(2)}, u32[]{:S(2)}) collective-permute-start(f32[1,3,1,1024]{3,2,1,0:T(1,128)S(1)} %get-tuple-element.192), channel_id=1, source_target_pairs={{0,1},{2,3},{4,5},{6,7},{8,9},{10,11},{12,13},{14,15},{16,17},{18,... | collective-permute-start | bytes 36872 | tf_op jit(solution)/shard_map/ppermute | solution.py:21
  82.7 4.3 %collective-permute-start.9 = (f32[1,3,4,1024]{3,2,1,0:T(4,128)S(1)}, f32[1,3,4,1024]{3,2,1,0:T(4,128)S(1)}, u32[]{:S(2)}, u32[]{:S(2)}) collective-permute-start(f32[1,3,4,1024]{3,2,1,0:T(4,128)S(1)} %get-tuple-element.191), channel_id=1, source_target_pairs={{1,0},{3,2},{5,4},{7,6},{9,8},{11,10},{13,12},{15,14},{17,16},{19,... | collective-permute-start | bytes 147464 | tf_op jit(solution)/shard_map/ppermute | solution.py:22
  84.0 3.9 %collective-permute-start.8 = (f32[1,3,4,1024]{3,2,1,0:T(4,128)S(1)}, f32[1,3,4,1024]{3,2,1,0:T(4,128)S(1)}, u32[]{:S(2)}, u32[]{:S(2)}) collective-permute-start(f32[1,3,4,1024]{3,2,1,0:T(4,128)S(1)} %get-tuple-element.190), channel_id=1, source_target_pairs={{0,1},{2,3},{4,5},{6,7},{8,9},{10,11},{12,13},{14,15},{16,17},{18,... | collective-permute-start | bytes 147464 | tf_op jit(solution)/shard_map/ppermute | solution.py:21
  91.5 5.2 %collective-permute-start.11 = (f32[2,3,4,1024]{3,2,1,0:T(4,128)S(1)}, f32[2,3,4,1024]{3,2,1,0:T(4,128)S(1)}, u32[]{:S(2)}, u32[]{:S(2)}) collective-permute-start(f32[2,3,4,1024]{3,2,1,0:T(4,128)S(1)} %get-tuple-element.89), channel_id=1, source_target_pairs={{1,0},{3,2},{5,4},{7,6},{9,8},{11,10},{13,12},{15,14},{17,16},{19,... | collective-permute-start | bytes 294920 | tf_op jit(solution)/shard_map/ppermute | solution.py:22
  92.8 4.0 %collective-permute-start.10 = (f32[2,3,4,1024]{3,2,1,0:T(4,128)S(1)}, f32[2,3,4,1024]{3,2,1,0:T(4,128)S(1)}, u32[]{:S(2)}, u32[]{:S(2)}) collective-permute-start(f32[2,3,4,1024]{3,2,1,0:T(4,128)S(1)} %get-tuple-element.88), channel_id=1, source_target_pairs={{0,1},{2,3},{4,5},{6,7},{8,9},{10,11},{12,13},{14,15},{16,17},{18,... | collective-permute-start | bytes 294920 | tf_op jit(solution)/shard_map/ppermute | solution.py:21
  101.6 258.3 %all-reduce.5.cloned.1.call-start = ((), (), s32[]{:S(2)}) async-start(), calls=%async_computation.1 | async-start | bytes 786432 | tf_op jit(solution)/shard_map/psum | solution.py:149
  207.8 4.3 %collective-permute-start.13 = (f32[1,3,4,1024]{3,2,1,0:T(4,128)S(1)}, f32[1,3,4,1024]{3,2,1,0:T(4,128)S(1)}, u32[]{:S(2)}, u32[]{:S(2)}) collective-permute-start(f32[1,3,4,1024]{3,2,1,0:T(4,128)S(1)} %get-tuple-element.189), channel_id=1, source_target_pairs={{1,0},{3,2},{5,4},{7,6},{9,8},{11,10},{13,12},{15,14},{17,16},{19,... | collective-permute-start | bytes 147464 | tf_op jit(solution)/shard_map/ppermute | solution.py:22
  209.1 3.9 %collective-permute-start.12 = (f32[1,3,4,1024]{3,2,1,0:T(4,128)S(1)}, f32[1,3,4,1024]{3,2,1,0:T(4,128)S(1)}, u32[]{:S(2)}, u32[]{:S(2)}) collective-permute-start(f32[1,3,4,1024]{3,2,1,0:T(4,128)S(1)} %get-tuple-element.188), channel_id=1, source_target_pairs={{0,1},{2,3},{4,5},{6,7},{8,9},{10,11},{12,13},{14,15},{16,17},{18,... | collective-permute-start | bytes 147464 | tf_op jit(solution)/shard_map/ppermute | solution.py:21
  216.6 4.3 %collective-permute-start.15 = (f32[2,3,4,1024]{3,2,1,0:T(4,128)S(1)}, f32[2,3,4,1024]{3,2,1,0:T(4,128)S(1)}, u32[]{:S(2)}, u32[]{:S(2)}) collective-permute-start(f32[2,3,4,1024]{3,2,1,0:T(4,128)S(1)} %get-tuple-element.87), channel_id=1, source_target_pairs={{1,0},{3,2},{5,4},{7,6},{9,8},{11,10},{13,12},{15,14},{17,16},{19,... | collective-permute-start | bytes 294920 | tf_op jit(solution)/shard_map/ppermute | solution.py:22
  217.9 4.0 %collective-permute-start.14 = (f32[2,3,4,1024]{3,2,1,0:T(4,128)S(1)}, f32[2,3,4,1024]{3,2,1,0:T(4,128)S(1)}, u32[]{:S(2)}, u32[]{:S(2)}) collective-permute-start(f32[2,3,4,1024]{3,2,1,0:T(4,128)S(1)} %get-tuple-element.86), channel_id=1, source_target_pairs={{0,1},{2,3},{4,5},{6,7},{8,9},{10,11},{12,13},{14,15},{16,17},{18,... | collective-permute-start | bytes 294920 | tf_op jit(solution)/shard_map/ppermute | solution.py:21
  227.0 4.3 %collective-permute-start.17 = (f32[1,3,1,1024]{3,2,1,0:T(1,128)S(1)}, f32[1,3,1,1024]{3,2,1,0:T(1,128)S(1)}, u32[]{:S(2)}, u32[]{:S(2)}) collective-permute-start(f32[1,3,1,1024]{3,2,1,0:T(1,128)S(1)} %get-tuple-element.187), channel_id=1, source_target_pairs={{1,0},{3,2},{5,4},{7,6},{9,8},{11,10},{13,12},{15,14},{17,16},{19,... | collective-permute-start | bytes 36872 | tf_op jit(solution)/shard_map/ppermute | solution.py:22
  228.3 3.9 %collective-permute-start.16 = (f32[1,3,1,1024]{3,2,1,0:T(1,128)S(1)}, f32[1,3,1,1024]{3,2,1,0:T(1,128)S(1)}, u32[]{:S(2)}, u32[]{:S(2)}) collective-permute-start(f32[1,3,1,1024]{3,2,1,0:T(1,128)S(1)} %get-tuple-element.186), channel_id=1, source_target_pairs={{0,1},{2,3},{4,5},{6,7},{8,9},{10,11},{12,13},{14,15},{16,17},{18,... | collective-permute-start | bytes 36872 | tf_op jit(solution)/shard_map/ppermute | solution.py:21
  233.2 4.6 %collective-permute-start.19 = (f32[1,3,4,1024]{3,2,1,0:T(4,128)S(1)}, f32[1,3,4,1024]{3,2,1,0:T(4,128)S(1)}, u32[]{:S(2)}, u32[]{:S(2)}) collective-permute-start(f32[1,3,4,1024]{3,2,1,0:T(4,128)S(1)} %get-tuple-element.185), channel_id=1, source_target_pairs={{1,0},{3,2},{5,4},{7,6},{9,8},{11,10},{13,12},{15,14},{17,16},{19,... | collective-permute-start | bytes 147464 | tf_op jit(solution)/shard_map/ppermute | solution.py:22
  234.5 3.9 %collective-permute-start.18 = (f32[1,3,4,1024]{3,2,1,0:T(4,128)S(1)}, f32[1,3,4,1024]{3,2,1,0:T(4,128)S(1)}, u32[]{:S(2)}, u32[]{:S(2)}) collective-permute-start(f32[1,3,4,1024]{3,2,1,0:T(4,128)S(1)} %get-tuple-element.184), channel_id=1, source_target_pairs={{0,1},{2,3},{4,5},{6,7},{8,9},{10,11},{12,13},{14,15},{16,17},{18,... | collective-permute-start | bytes 147464 | tf_op jit(solution)/shard_map/ppermute | solution.py:21
  241.9 4.3 %collective-permute-start.21 = (f32[2,3,4,1024]{3,2,1,0:T(4,128)S(1)}, f32[2,3,4,1024]{3,2,1,0:T(4,128)S(1)}, u32[]{:S(2)}, u32[]{:S(2)}) collective-permute-start(f32[2,3,4,1024]{3,2,1,0:T(4,128)S(1)} %get-tuple-element.85), channel_id=1, source_target_pairs={{1,0},{3,2},{5,4},{7,6},{9,8},{11,10},{13,12},{15,14},{17,16},{19,... | collective-permute-start | bytes 294920 | tf_op jit(solution)/shard_map/ppermute | solution.py:22
  243.2 4.0 %collective-permute-start.20 = (f32[2,3,4,1024]{3,2,1,0:T(4,128)S(1)}, f32[2,3,4,1024]{3,2,1,0:T(4,128)S(1)}, u32[]{:S(2)}, u32[]{:S(2)}) collective-permute-start(f32[2,3,4,1024]{3,2,1,0:T(4,128)S(1)} %get-tuple-element.84), channel_id=1, source_target_pairs={{0,1},{2,3},{4,5},{6,7},{8,9},{10,11},{12,13},{14,15},{16,17},{18,... | collective-permute-start | bytes 294920 | tf_op jit(solution)/shard_map/ppermute | solution.py:21
  (4 other events, 118.0 us)
Sparse Core Ops, SparseCore 0:
  101.7 104.7 all-reduce.2
  252.1 107.7 all-reduce.4
where the time goes:
time: 369 us; the launch traced here: 368 us
  waiting for transfers between devices  219 us (59%)
  starting transfers between devices  48.2 us (13%)
  blocking collectives  45.3 us (12%)
  other arithmetic  21.8 us (6%)
  between operations  17.7 us (5%)
  local copies, waits for them, and re-layouts  16.1 us (4%)
    psum x2, waiting for transfers between devices, summed_whole(): return lax.psum(partial_value, 'phase')  213 us
    all_gather x1, blocking collectives, per_device(): whole_tile = lax.all_gather(state_now, 'phase', axis=1, tiled=True)  45.3 us
    ppermute x11, starting transfers between devices, extended(): before = lax.ppermute(last, axis, up)  33.8 us
    ppermute x11, starting transfers between devices, extended(): after = lax.ppermute(first, axis, down)  14.3 us
    slice x140, local copies, waits for them, and re-layouts, along_lon(): return (jnp.roll(values, -1, axis=-1) - jnp.roll(values, 1, axis=-1)) * 0.5  12.7 us
    another operation x63, other arithmetic, wave_operator(): return jnp.stack([out_height, out_east, out_north], axis=1) / radius_scale  7.91 us
  transfers between devices with their start and end apart: 24, of which 10 were waited for; matrix products, arithmetic and copies ran while one was open for 0% of the time, Pallas kernels for 0%

commit v1 on v0

--- a/solution.py
+++ b/solution.py
@@ -3,6 +3,7 @@
 import jax.numpy as jnp
 from jax import lax
 from jax.sharding import PartitionSpec as P
+from jax.lax import all_gather
 
 DEG = 8
 DEPTH = 4
@@ -143,7 +144,10 @@
         returned = exponential(pulled, backward)
         return jnp.sum(phase_weights[:, None, None, None] * returned, axis=0)
 
-    whole_tile = lax.all_gather(state_now, "phase", axis=1, tiled=True)
+    def _press_local_data(w_in, device_axis, where_dim):
+        return jnp.concatenate(all_gather(w_in, device_axis), axis=where_dim)
+
+    whole_tile = _press_local_data(state_now, "phase", 1)
 
     def summed_whole(partial_value):
         return lax.psum(partial_value, "phase")

time: 369 us -> 367 us (level)
  no operation moved by 1% of the time
where the time goes in v1:
time: 367 us; the launch traced here: 366 us
  waiting for transfers between devices  219 us (60%)
  starting transfers between devices  48.2 us (13%)
  blocking collectives  44.7 us (12%)
  other arithmetic  21.2 us (6%)
  between operations  17.7 us (5%)
  local copies, waits for them, and re-layouts  15.7 us (4%)
    psum x2, waiting for transfers between devices, summed_whole(): return lax.psum(partial_value, 'phase')  212 us
    all_gather x1, blocking collectives, _press_local_data(): return jnp.concatenate(all_gather(w_in, device_axis), axis=where_dim)  44.7 us
    ppermute x11, starting transfers between devices, extended(): before = lax.ppermute(last, axis, up)  33.8 us
    ppermute x11, starting transfers between devices, extended(): after = lax.ppermute(first, axis, down)  14.3 us
    slice x140, local copies, waits for them, and re-layouts, along_lon(): return (jnp.roll(values, -1, axis=-1) - jnp.roll(values, 1, axis=-1)) * 0.5  12.7 us
    another operation x63, other arithmetic, wave_operator(): return jnp.stack([out_height, out_east, out_north], axis=1) / radius_scale  7.92 us
  transfers between devices with their start and end apart: 24, of which 10 were waited for; matrix products, arithmetic and copies ran while one was open for 0% of the time, Pallas kernels for 0%

profile of v1, /device:TPU:0, one launch (start us, length us, event | category | flops | bytes accessed | tf_op | source)
XLA Modules:
  0.0 366.4 jit_solution(15152447900863589484)
XLA Ops:
  7.2 44.7 %all-gather = f32[48,2,1024]{2,1,0:T(2,128)S(1)} all-gather(f32[3,2,1024]{2,1,0:T(2,128)} %param.5), channel_id=2, replica_groups=mesh['phase'=16,'lat'=2] {'phase'}, dimensions={0}, use_global_device_ids=true | all-gather | bytes 417792 | tf_op jit(solution)/shard_map/all_gather | solution.py:148
  52.3 1.4 collective-permute-start.3
  53.8 3.0 collective-permute-start.2
  56.9 1.3 collective-permute-start.1
  58.2 3.0 collective-permute-start
  65.7 1.3 collective-permute-start.5
  67.0 3.0 collective-permute-start.4
  75.1 1.3 collective-permute-start.7
  76.4 3.0 collective-permute-start.6
  81.3 1.3 collective-permute-start.9
  82.6 3.0 collective-permute-start.8
  90.0 1.3 collective-permute-start.11
  91.3 3.2 collective-permute-start.10
  98.8 1.3 fusion.41
  100.4 104.6 %all-reduce.3.cloned.1.call-done = f32[3,32,1024]{2,1,0:T(8,128)} async-done(((f32[3,32,1024]{2,1,0:T(8,128)}), f32[3,32,1024]{2,1,0:T(8,128)}) %all-reduce.3.cloned.1.call-update) | async-done | bytes 393232 | tf_op jit(solution)/shard_map/psum | solution.py:153
  206.1 1.3 collective-permute-start.13
  207.4 3.0 collective-permute-start.12
  216.2 3.0 collective-permute-start.14
  226.5 3.0 collective-permute-start.16
  232.6 3.3 collective-permute-start.18
  240.1 1.3 collective-permute-start.21
  241.4 3.0 collective-permute-start.20
  250.2 107.9 %all-reduce.5.cloned.1.call-done = f32[3,32,1024]{2,1,0:T(8,128)} async-done(((f32[3,32,1024]{2,1,0:T(8,128)}), f32[3,32,1024]{2,1,0:T(8,128)}) %all-reduce.5.cloned.1.call-update) | async-done | bytes 393232 | tf_op jit(solution)/shard_map/psum | solution.py:153
  358.1 1.5 multiply_add_fusion.1
  (381 shorter events, 44.4 us)
Async XLA Ops:
  7.2 197.9 %all-reduce.3.cloned.1.call-start = ((), (), s32[]{:S(2)}) async-start(), calls=%async_computation | async-start | bytes 786432 | tf_op jit(solution)/shard_map/psum | solution.py:153
  52.3 9.8 %collective-permute-start.3 = (f32[1,3,4,1024]{3,2,1,0:T(4,128)S(1)}, f32[1,3,4,1024]{3,2,1,0:T(4,128)S(1)}, u32[]{:S(2)}, u32[]{:S(2)}) collective-permute-start(f32[1,3,4,1024]{3,2,1,0:T(4,128)S(1)} %get-tuple-element.195), channel_id=1, source_target_pairs={{1,0},{3,2},{5,4},{7,6},{9,8},{11,10},{13,12},{15,14},{17,16},{19,... | collective-permute-start | bytes 147464 | tf_op jit(solution)/shard_map/ppermute | solution.py:23
  53.8 8.4 %collective-permute-start.2 = (f32[1,3,4,1024]{3,2,1,0:T(4,128)S(1)}, f32[1,3,4,1024]{3,2,1,0:T(4,128)S(1)}, u32[]{:S(2)}, u32[]{:S(2)}) collective-permute-start(f32[1,3,4,1024]{3,2,1,0:T(4,128)S(1)} %get-tuple-element.194), channel_id=1, source_target_pairs={{0,1},{2,3},{4,5},{6,7},{8,9},{10,11},{12,13},{14,15},{16,17},{18,... | collective-permute-start | bytes 147464 | tf_op jit(solution)/shard_map/ppermute | solution.py:22
  56.9 4.6 %collective-permute-start.1 = (f32[2,4,1024]{2,1,0:T(4,128)S(1)}, f32[2,4,1024]{2,1,0:T(4,128)S(1)}, u32[]{:S(2)}, u32[]{:S(2)}) collective-permute-start(f32[2,4,1024]{2,1,0:T(4,128)S(1)} %get-tuple-element.205), channel_id=1, source_target_pairs={{1,0},{3,2},{5,4},{7,6},{9,8},{11,10},{13,12},{15,14},{17,16},{19,... | collective-permute-start | bytes 98312 | tf_op jit(solution)/shard_map/ppermute | solution.py:23
  58.2 3.9 %collective-permute-start = (f32[2,4,1024]{2,1,0:T(4,128)S(1)}, f32[2,4,1024]{2,1,0:T(4,128)S(1)}, u32[]{:S(2)}, u32[]{:S(2)}) collective-permute-start(f32[2,4,1024]{2,1,0:T(4,128)S(1)} %get-tuple-element.204), channel_id=1, source_target_pairs={{0,1},{2,3},{4,5},{6,7},{8,9},{10,11},{12,13},{14,15},{16,17},{18,... | collective-permute-start | bytes 98312 | tf_op jit(solution)/shard_map/ppermute | solution.py:22
  65.7 5.3 %collective-permute-start.5 = (f32[2,3,4,1024]{3,2,1,0:T(4,128)S(1)}, f32[2,3,4,1024]{3,2,1,0:T(4,128)S(1)}, u32[]{:S(2)}, u32[]{:S(2)}) collective-permute-start(f32[2,3,4,1024]{3,2,1,0:T(4,128)S(1)} %get-tuple-element.91), channel_id=1, source_target_pairs={{1,0},{3,2},{5,4},{7,6},{9,8},{11,10},{13,12},{15,14},{17,16},{19,... | collective-permute-start | bytes 294920 | tf_op jit(solution)/shard_map/ppermute | solution.py:23
  67.0 4.0 %collective-permute-start.4 = (f32[2,3,4,1024]{3,2,1,0:T(4,128)S(1)}, f32[2,3,4,1024]{3,2,1,0:T(4,128)S(1)}, u32[]{:S(2)}, u32[]{:S(2)}) collective-permute-start(f32[2,3,4,1024]{3,2,1,0:T(4,128)S(1)} %get-tuple-element.90), channel_id=1, source_target_pairs={{0,1},{2,3},{4,5},{6,7},{8,9},{10,11},{12,13},{14,15},{16,17},{18,... | collective-permute-start | bytes 294920 | tf_op jit(solution)/shard_map/ppermute | solution.py:22
  75.1 4.3 %collective-permute-start.7 = (f32[1,3,1,1024]{3,2,1,0:T(1,128)S(1)}, f32[1,3,1,1024]{3,2,1,0:T(1,128)S(1)}, u32[]{:S(2)}, u32[]{:S(2)}) collective-permute-start(f32[1,3,1,1024]{3,2,1,0:T(1,128)S(1)} %get-tuple-element.193), channel_id=1, source_target_pairs={{1,0},{3,2},{5,4},{7,6},{9,8},{11,10},{13,12},{15,14},{17,16},{19,... | collective-permute-start | bytes 36872 | tf_op jit(solution)/shard_map/ppermute | solution.py:23
  76.4 3.9 %collective-permute-start.6 = (f32[1,3,1,1024]{3,2,1,0:T(1,128)S(1)}, f32[1,3,1,1024]{3,2,1,0:T(1,128)S(1)}, u32[]{:S(2)}, u32[]{:S(2)}) collective-permute-start(f32[1,3,1,1024]{3,2,1,0:T(1,128)S(1)} %get-tuple-element.192), channel_id=1, source_target_pairs={{0,1},{2,3},{4,5},{6,7},{8,9},{10,11},{12,13},{14,15},{16,17},{18,... | collective-permute-start | bytes 36872 | tf_op jit(solution)/shard_map/ppermute | solution.py:22
  81.3 4.3 %collective-permute-start.9 = (f32[1,3,4,1024]{3,2,1,0:T(4,128)S(1)}, f32[1,3,4,1024]{3,2,1,0:T(4,128)S(1)}, u32[]{:S(2)}, u32[]{:S(2)}) collective-permute-start(f32[1,3,4,1024]{3,2,1,0:T(4,128)S(1)} %get-tuple-element.191), channel_id=1, source_target_pairs={{1,0},{3,2},{5,4},{7,6},{9,8},{11,10},{13,12},{15,14},{17,16},{19,... | collective-permute-start | bytes 147464 | tf_op jit(solution)/shard_map/ppermute | solution.py:23
  82.6 3.9 %collective-permute-start.8 = (f32[1,3,4,1024]{3,2,1,0:T(4,128)S(1)}, f32[1,3,4,1024]{3,2,1,0:T(4,128)S(1)}, u32[]{:S(2)}, u32[]{:S(2)}) collective-permute-start(f32[1,3,4,1024]{3,2,1,0:T(4,128)S(1)} %get-tuple-element.190), channel_id=1, source_target_pairs={{0,1},{2,3},{4,5},{6,7},{8,9},{10,11},{12,13},{14,15},{16,17},{18,... | collective-permute-start | bytes 147464 | tf_op jit(solution)/shard_map/ppermute | solution.py:22
  90.0 5.2 %collective-permute-start.11 = (f32[2,3,4,1024]{3,2,1,0:T(4,128)S(1)}, f32[2,3,4,1024]{3,2,1,0:T(4,128)S(1)}, u32[]{:S(2)}, u32[]{:S(2)}) collective-permute-start(f32[2,3,4,1024]{3,2,1,0:T(4,128)S(1)} %get-tuple-element.89), channel_id=1, source_target_pairs={{1,0},{3,2},{5,4},{7,6},{9,8},{11,10},{13,12},{15,14},{17,16},{19,... | collective-permute-start | bytes 294920 | tf_op jit(solution)/shard_map/ppermute | solution.py:23
  91.3 4.0 %collective-permute-start.10 = (f32[2,3,4,1024]{3,2,1,0:T(4,128)S(1)}, f32[2,3,4,1024]{3,2,1,0:T(4,128)S(1)}, u32[]{:S(2)}, u32[]{:S(2)}) collective-permute-start(f32[2,3,4,1024]{3,2,1,0:T(4,128)S(1)} %get-tuple-element.88), channel_id=1, source_target_pairs={{0,1},{2,3},{4,5},{6,7},{8,9},{10,11},{12,13},{14,15},{16,17},{18,... | collective-permute-start | bytes 294920 | tf_op jit(solution)/shard_map/ppermute | solution.py:22
  100.1 257.9 %all-reduce.5.cloned.1.call-start = ((), (), s32[]{:S(2)}) async-start(), calls=%async_computation.1 | async-start | bytes 786432 | tf_op jit(solution)/shard_map/psum | solution.py:153
  206.1 4.3 %collective-permute-start.13 = (f32[1,3,4,1024]{3,2,1,0:T(4,128)S(1)}, f32[1,3,4,1024]{3,2,1,0:T(4,128)S(1)}, u32[]{:S(2)}, u32[]{:S(2)}) collective-permute-start(f32[1,3,4,1024]{3,2,1,0:T(4,128)S(1)} %get-tuple-element.189), channel_id=1, source_target_pairs={{1,0},{3,2},{5,4},{7,6},{9,8},{11,10},{13,12},{15,14},{17,16},{19,... | collective-permute-start | bytes 147464 | tf_op jit(solution)/shard_map/ppermute | solution.py:23
  207.4 3.9 %collective-permute-start.12 = (f32[1,3,4,1024]{3,2,1,0:T(4,128)S(1)}, f32[1,3,4,1024]{3,2,1,0:T(4,128)S(1)}, u32[]{:S(2)}, u32[]{:S(2)}) collective-permute-start(f32[1,3,4,1024]{3,2,1,0:T(4,128)S(1)} %get-tuple-element.188), channel_id=1, source_target_pairs={{0,1},{2,3},{4,5},{6,7},{8,9},{10,11},{12,13},{14,15},{16,17},{18,... | collective-permute-start | bytes 147464 | tf_op jit(solution)/shard_map/ppermute | solution.py:22
  214.9 4.3 %collective-permute-start.15 = (f32[2,3,4,1024]{3,2,1,0:T(4,128)S(1)}, f32[2,3,4,1024]{3,2,1,0:T(4,128)S(1)}, u32[]{:S(2)}, u32[]{:S(2)}) collective-permute-start(f32[2,3,4,1024]{3,2,1,0:T(4,128)S(1)} %get-tuple-element.87), channel_id=1, source_target_pairs={{1,0},{3,2},{5,4},{7,6},{9,8},{11,10},{13,12},{15,14},{17,16},{19,... | collective-permute-start | bytes 294920 | tf_op jit(solution)/shard_map/ppermute | solution.py:23
  216.2 4.0 %collective-permute-start.14 = (f32[2,3,4,1024]{3,2,1,0:T(4,128)S(1)}, f32[2,3,4,1024]{3,2,1,0:T(4,128)S(1)}, u32[]{:S(2)}, u32[]{:S(2)}) collective-permute-start(f32[2,3,4,1024]{3,2,1,0:T(4,128)S(1)} %get-tuple-element.86), channel_id=1, source_target_pairs={{0,1},{2,3},{4,5},{6,7},{8,9},{10,11},{12,13},{14,15},{16,17},{18,... | collective-permute-start | bytes 294920 | tf_op jit(solution)/shard_map/ppermute | solution.py:22
  225.2 4.3 %collective-permute-start.17 = (f32[1,3,1,1024]{3,2,1,0:T(1,128)S(1)}, f32[1,3,1,1024]{3,2,1,0:T(1,128)S(1)}, u32[]{:S(2)}, u32[]{:S(2)}) collective-permute-start(f32[1,3,1,1024]{3,2,1,0:T(1,128)S(1)} %get-tuple-element.187), channel_id=1, source_target_pairs={{1,0},{3,2},{5,4},{7,6},{9,8},{11,10},{13,12},{15,14},{17,16},{19,... | collective-permute-start | bytes 36872 | tf_op jit(solution)/shard_map/ppermute | solution.py:23
  226.5 3.9 %collective-permute-start.16 = (f32[1,3,1,1024]{3,2,1,0:T(1,128)S(1)}, f32[1,3,1,1024]{3,2,1,0:T(1,128)S(1)}, u32[]{:S(2)}, u32[]{:S(2)}) collective-permute-start(f32[1,3,1,1024]{3,2,1,0:T(1,128)S(1)} %get-tuple-element.186), channel_id=1, source_target_pairs={{0,1},{2,3},{4,5},{6,7},{8,9},{10,11},{12,13},{14,15},{16,17},{18,... | collective-permute-start | bytes 36872 | tf_op jit(solution)/shard_map/ppermute | solution.py:22
  231.3 4.6 %collective-permute-start.19 = (f32[1,3,4,1024]{3,2,1,0:T(4,128)S(1)}, f32[1,3,4,1024]{3,2,1,0:T(4,128)S(1)}, u32[]{:S(2)}, u32[]{:S(2)}) collective-permute-start(f32[1,3,4,1024]{3,2,1,0:T(4,128)S(1)} %get-tuple-element.185), channel_id=1, source_target_pairs={{1,0},{3,2},{5,4},{7,6},{9,8},{11,10},{13,12},{15,14},{17,16},{19,... | collective-permute-start | bytes 147464 | tf_op jit(solution)/shard_map/ppermute | solution.py:23
  232.6 3.9 %collective-permute-start.18 = (f32[1,3,4,1024]{3,2,1,0:T(4,128)S(1)}, f32[1,3,4,1024]{3,2,1,0:T(4,128)S(1)}, u32[]{:S(2)}, u32[]{:S(2)}) collective-permute-start(f32[1,3,4,1024]{3,2,1,0:T(4,128)S(1)} %get-tuple-element.184), channel_id=1, source_target_pairs={{0,1},{2,3},{4,5},{6,7},{8,9},{10,11},{12,13},{14,15},{16,17},{18,... | collective-permute-start | bytes 147464 | tf_op jit(solution)/shard_map/ppermute | solution.py:22
  240.1 4.3 %collective-permute-start.21 = (f32[2,3,4,1024]{3,2,1,0:T(4,128)S(1)}, f32[2,3,4,1024]{3,2,1,0:T(4,128)S(1)}, u32[]{:S(2)}, u32[]{:S(2)}) collective-permute-start(f32[2,3,4,1024]{3,2,1,0:T(4,128)S(1)} %get-tuple-element.85), channel_id=1, source_target_pairs={{1,0},{3,2},{5,4},{7,6},{9,8},{11,10},{13,12},{15,14},{17,16},{19,... | collective-permute-start | bytes 294920 | tf_op jit(solution)/shard_map/ppermute | solution.py:23
  241.4 4.0 %collective-permute-start.20 = (f32[2,3,4,1024]{3,2,1,0:T(4,128)S(1)}, f32[2,3,4,1024]{3,2,1,0:T(4,128)S(1)}, u32[]{:S(2)}, u32[]{:S(2)}) collective-permute-start(f32[2,3,4,1024]{3,2,1,0:T(4,128)S(1)} %get-tuple-element.84), channel_id=1, source_target_pairs={{0,1},{2,3},{4,5},{6,7},{8,9},{10,11},{12,13},{14,15},{16,17},{18,... | collective-permute-start | bytes 294920 | tf_op jit(solution)/shard_map/ppermute | solution.py:22
  (4 other events, 118.0 us)
Sparse Core Ops, SparseCore 0:
  100.2 104.7 all-reduce.2
  250.3 107.7 all-reduce.4
